TPU v7x, 32 devices: a whole 2x2x4 slice. The times are simulated.
32 devices in a mesh: grp: 4 (over y, core), blk: 8 (over z, x).
Axes of the slice: x: 2, y: 2, z: 4, core: 2. Of those that a mesh axis runs over, the one named last changes fastest.
Arguments:
- generator: bfloat16 [4, 16384, 2560], P('grp', 'blk'), may hold values from -0.125 to 0.125
- eta_mask: int32 [4, 128, 20], P('grp', 'blk'), may hold values from 0 to 1
- pair_tiles: bfloat16 [4, 8, 20, 128, 128], P('grp', 'blk'), may hold values from -6 to 6
- tile_order: int32 [4, 8, 20], P('grp', 'blk'), may hold values from 0 to 19, each once within a row
- tile_phase: int32 [4, 8, 20], P('grp', 'blk'), may hold values from 0 to 1
- occupation: float32 [4, 2560], P('grp'), may hold values from -1 to 1
- channel_sign: int32 [4, 4], replicated, may hold values from 0 to 1
- swap_perm: int32 [4, 8, 256], P('grp', 'blk'), may hold values from 0 to 255, each once within a row
Outputs:
- result: float32 [4, 16384, 256], P('grp', 'blk')
Inputs may be any that keep to these rules, and one draw needn't show every extreme that they name: `tile_order`: each device's list names each of its 20 held tiles once. `swap_perm`: each device's row names each of its 256 columns once.
All inputs are finite; a program needn't handle non-finite values.
Results may differ from a plain program's by a relative error of at most 0.004.
Values may be sent and summed in bfloat16 or wider, within the bound.
A program may use at most 128 MiB of HBM per device.

v0:
```python
import jax
import jax.numpy as jnp
from jax import lax
from jax.sharding import PartitionSpec as P

BAND = 8


def passed_along(value, axis, steps):
    count = lax.axis_size(axis)
    pairs = [(source, (source + steps) % count) for source in range(count)]
    return lax.ppermute(value, axis, pairs)


def shards(
    generator, eta_mask, pair_tiles, tile_order, tile_phase, occupation, channel_sign, swap_perm
):
    tile_size = pair_tiles.shape[-1]
    tile_count = pair_tiles.shape[2]
    pair_width = generator.shape[2]
    row_count = generator.shape[1]
    half_band = BAND // 2
    chosen = jnp.take(pair_tiles[0, 0], tile_order[0, 0], axis=0)
    phases = (1 - 2 * tile_phase[0, 0]).astype(jnp.bfloat16)
    outgoing = chosen * phases[:, None, None]
    arrived = lax.all_to_all(outgoing, "grp", split_axis=0, concat_axis=0, tiled=True)
    gathered = arrived.reshape(pair_width, tile_size)
    scaled = (occupation[0][:, None] * gathered.astype(jnp.float32)).astype(jnp.bfloat16)
    shaped = generator[0].reshape(row_count // tile_size, tile_size, tile_count, tile_size)
    kept_mask = eta_mask[0].astype(jnp.bfloat16)
    masked = (shaped * kept_mask[:, None, :, None]).reshape(row_count, pair_width)
    below_list = []
    travelling = scaled
    for hop_index in range(half_band):
        travelling = passed_along(travelling, "blk", 1)
        below_list.append(travelling)
    above_list = []
    travelling = scaled
    for hop_index in range(half_band - 1):
        travelling = passed_along(travelling, "blk", -1)
        above_list.append(travelling)
    band_pieces = below_list[::-1] + [scaled] + above_list
    band_matrix = jnp.concatenate(band_pieces, axis=1)
    product_block = jnp.dot(masked, band_matrix, preferred_element_type=jnp.float32).astype(
        jnp.bfloat16
    )
    returned = lax.all_to_all(product_block[None], "grp", split_axis=2, concat_axis=0, tiled=True)
    my_group = lax.axis_index("grp")
    sign_row = lax.dynamic_index_in_dim(channel_sign, my_group, 0, keepdims=False)
    sign_values = (1 - 2 * sign_row).astype(jnp.float32)
    summed = jnp.sum(sign_values[:, None, None] * returned.astype(jnp.float32), axis=0)
    partner = jnp.take(summed, swap_perm[0, 0], axis=1)
    return (summed - partner)[None]


def solution(mesh):
    return jax.shard_map(
        shards,
        mesh=mesh,
        in_specs=(
            P("grp", "blk", None),
            P("grp", "blk", None),
            P("grp", "blk", None, None, None),
            P("grp", "blk", None),
            P("grp", "blk", None),
            P("grp", None),
            P(),
            P("grp", "blk", None),
        ),
        out_specs=P("grp", "blk", None),
        check_vma=False,
    )
```

profile of v0, /device:TPU:1, one launch (start us, length us, event | category | flops | bytes accessed | tf_op | source)
XLA Modules:
  0.0 312.3 jit_solution(151206699576998182)
XLA Ops:
  0.0 0.0 copy-start
  0.0 0.0 copy-start.3
  0.0 0.7 fusion.6
  0.7 0.7 compare_and_fusion.1
  1.4 0.7 compare_select_fusion
  2.1 0.7 convert_bitcast_fusion.2
  2.7 0.0 copy-done
  2.7 0.7 gather_fusion
  3.4 1.0 select_multiply_fusion
  4.4 4.3 %all-to-all-start = ((bf16[20,128,128]{2,1,0:T(8,128)(2,1)}), bf16[20,128,128]{2,1,0:T(8,128)(2,1)S(1)}, u32[]{:S(2)}, u32[]{:S(2)}) async-start(bf16[20,128,128]{2,1,0:T(8,128)(2,1)} %select_multiply_fusion), calls=%async_computation | async-start | bytes 1310720 | tf_op jit(solution)/shard_map/all_to_all | solution.py:26
  8.7 0.7 reduce
  9.4 8.3 %all-to-all-done = bf16[20,128,128]{2,1,0:T(8,128)(2,1)S(1)} async-done(((bf16[20,128,128]{2,1,0:T(8,128)(2,1)}), bf16[20,128,128]{2,1,0:T(8,128)(2,1)S(1)}, u32[]{:S(2)}, u32[]{:S(2)}) %all-to-all-start) | async-done | bytes 655392 | tf_op jit(solution)/shard_map/all_to_all | solution.py:26
  17.8 0.4 fusion.5
  18.2 2.1 collective-permute-start
  20.3 17.2 %collective-permute-done = bf16[2560,128]{1,0:T(8,128)(2,1)S(1)} collective-permute-done((bf16[2560,128]{1,0:T(8,128)(2,1)S(1)}, bf16[2560,128]{1,0:T(8,128)(2,1)S(1)}, u32[]{:S(2)}, u32[]{:S(2)}) %collective-permute-start) | collective-permute-done | bytes 655392 | tf_op jit(solution)/shard_map/ppermute | solution.py:12
  37.5 0.0 collective-permute-start.1
  37.5 4.2 %collective-permute-start.4 = (bf16[2560,128]{1,0:T(8,128)(2,1)S(1)}, bf16[2560,128]{1,0:T(8,128)(2,1)S(1)}, u32[]{:S(2)}, u32[]{:S(2)}) collective-permute-start(bf16[2560,128]{1,0:T(8,128)(2,1)S(1)} %fusion.5), channel_id=1, source_target_pairs={{0,7},{1,0},{2,1},{3,2},{4,3},{5,4},{6,5},{7,6},{8,15},{9,8},{10,9... | collective-permute-start | bytes 1966088 | tf_op jit(solution)/shard_map/ppermute | solution.py:12
  41.6 23.1 %collective-permute-done.1 = bf16[2560,128]{1,0:T(8,128)(2,1)S(1)} collective-permute-done((bf16[2560,128]{1,0:T(8,128)(2,1)S(1)}, bf16[2560,128]{1,0:T(8,128)(2,1)S(1)}, u32[]{:S(2)}, u32[]{:S(2)}) %collective-permute-start.1) | collective-permute-done | bytes 655392 | tf_op jit(solution)/shard_map/ppermute | solution.py:12
  64.8 2.2 collective-permute-start.2
  67.0 0.0 collective-permute-done.4
  67.0 16.3 %collective-permute-start.5 = (bf16[2560,128]{1,0:T(8,128)(2,1)S(1)}, bf16[2560,128]{1,0:T(8,128)(2,1)S(1)}, u32[]{:S(2)}, u32[]{:S(2)}) collective-permute-start(bf16[2560,128]{1,0:T(8,128)(2,1)S(1)} %collective-permute-done.4), channel_id=1, source_target_pairs={{0,7},{1,0},{2,1},{3,2},{4,3},{5,4},{6,5},{7,6},{8,15},{9,8},{10,9... | collective-permute-start | bytes 1966088 | tf_op jit(solution)/shard_map/ppermute | solution.py:12
  83.2 11.3 %collective-permute-done.2 = bf16[2560,128]{1,0:T(8,128)(2,1)} collective-permute-done((bf16[2560,128]{1,0:T(8,128)(2,1)S(1)}, bf16[2560,128]{1,0:T(8,128)(2,1)}, u32[]{:S(2)}, u32[]{:S(2)}) %collective-permute-start.2) | collective-permute-done | bytes 655392 | tf_op jit(solution)/shard_map/ppermute | solution.py:12
  94.5 2.3 collective-permute-start.3
  96.8 0.0 copy-done.3
  96.8 0.1 copy.14
  96.9 14.6 %copy.13 = bf16[1,2048,2560]{1,2,0:T(8,128)(2,1)} copy(bf16[1,2048,2560]{2,1,0:T(8,128)(2,1)} %param.8) | data formatting | bytes 20971520 | tf_op args[0]
  111.5 0.0 collective-permute-done.5
  111.5 1.9 collective-permute-start.6
  113.3 0.0 collective-permute-done.3
  113.3 2.0 constant_dynamic-update-slice_fusion.7
  115.4 2.1 constant_dynamic-update-slice_fusion.6
  117.4 1.0 constant_dynamic-update-slice_fusion.5
  118.4 0.9 constant_dynamic-update-slice_fusion.4
  119.3 0.9 constant_dynamic-update-slice_fusion.3
  120.2 0.9 constant_dynamic-update-slice_fusion.2
  121.2 0.9 constant_dynamic-update-slice_fusion.1
  122.1 3.9 %collective-permute-done.6 = bf16[2560,128]{1,0:T(8,128)(2,1)S(1)} collective-permute-done((bf16[2560,128]{1,0:T(8,128)(2,1)S(1)}, bf16[2560,128]{1,0:T(8,128)(2,1)S(1)}, u32[]{:S(2)}, u32[]{:S(2)}) %collective-permute-start.6) | collective-permute-done | bytes 655392 | tf_op jit(solution)/shard_map/ppermute | solution.py:12
  126.1 0.9 constant_dynamic-update-slice_fusion
  127.0 0.0 copy-start.2
  127.0 6.7 %mul.55 = bf16[16,128,20,128]{1,0,3,2:T(8,128)(2,1)} broadcast(bf16[16,20]{0,1:T(8,128)(2,1)S(1)} %copy.14), dimensions={0,2} | broadcast | bytes 10486400 | tf_op jit(solution)/shard_map/mul | solution.py:31
  133.7 1.0 copy-done.2
  134.7 17.0 %convert_bitcast_fusion = bf16[1,2048,1024]{2,1,0:T(8,128)(2,1)} fusion(bf16[2560,1024]{1,0:T(8,128)(2,1)} %constant_dynamic-update-slice_fusion, bf16[320,8,16,128]{3,2,1,0:T(8,128)(2,1)} %bitcast.60, bf16[1,2048,2560]{1,2,0:T(8,128)(2,1)S(1)} %copy-done.2), kind=kOutput, calls=%fused_computation.8 | convolution fusion | flops 10744758272 | bytes 30408704 | tf_op jit(solution)/shard_map/dot_general | solution.py:44
  151.8 20.6 %copy.15 = bf16[1,2048,1024]{1,0,2:T(2,128)(2,1)} copy(bf16[1,2048,1024]{2,1,0:T(8,128)(2,1)} %convert_bitcast_fusion) | data formatting | bytes 8388608 | tf_op jit(solution)/shard_map/broadcast_in_dim | solution.py:47
  172.4 0.5 broadcast.140
  172.9 26.7 %reduce.1 = bf16[1024,2048]{1,0:T(8,128)(2,1)} reduce(bf16[1024,1,2048]{2,1,0:T(2,128)(2,1)} %bitcast.58, bf16[]{:T(256)} %broadcast.140), dimensions={1}, to_apply=%bitcast.54.reduce_sub_computation | reduce | bytes 8388610
  199.6 6.3 %reshape.163 = bf16[4,2,262144]{2,1,0:T(2,128)(2,1)} reshape(bf16[1024,2048]{1,0:T(8,128)(2,1)} %reduce.1) | data formatting | bytes 8388608
  205.8 0.0 copy-start.4
  205.8 7.6 %all-to-all-start.1 = ((bf16[4,2,262144]{2,1,0:T(2,128)(2,1)}), bf16[4,2,262144]{2,1,0:T(2,128)(2,1)}, u32[]{:S(2)}, u32[]{:S(2)}) async-start(bf16[4,2,262144]{2,1,0:T(2,128)(2,1)} %reshape.163), calls=%async_computation.1 | async-start | bytes 8388608 | tf_op jit(solution)/shard_map/all_to_all | solution.py:47
  213.4 0.7 convert_bitcast_fusion.3
  214.1 0.0 copy-done.4
  214.1 46.6 %all-to-all-done.1 = bf16[4,2,262144]{2,1,0:T(2,128)(2,1)} async-done(((bf16[4,2,262144]{2,1,0:T(2,128)(2,1)}), bf16[4,2,262144]{2,1,0:T(2,128)(2,1)}, u32[]{:S(2)}, u32[]{:S(2)}) %all-to-all-start.1) | async-done | bytes 4194336 | tf_op jit(solution)/shard_map/all_to_all | solution.py:47
  260.7 7.4 %reshape.164 = bf16[1024,1,2048]{2,1,0:T(2,128)(2,1)} reshape(bf16[4,2,262144]{2,1,0:T(2,128)(2,1)} %all-to-all-done.1) | data formatting | bytes 8388608
  268.2 21.4 %copy.16 = f32[1,2048,4,256]{3,2,1,0:T(4,128)} copy(bf16[1,2048,4,256]{1,0,3,2:T(2,128)(2,1)} %bitcast.59) | data formatting | bytes 12582912 | tf_op jit(solution)/shard_map/convert_element_type | solution.py:51
  289.6 12.0 %fusion.3 = f32[2048,256]{1,0:T(8,128)} fusion(f32[1,2048,4,256]{3,2,1,0:T(4,128)} %copy.16, f32[4]{0:T(128)S(1)} %convert_bitcast_fusion.3), kind=kLoop, calls=%fused_computation.7 | loop fusion | flops 3670016 | bytes 10485776 | tf_op jit(solution)/shard_map/reduce_sum | solution.py:51
  301.6 1.9 copy.17
  303.5 0.0 copy-start.1
  303.5 2.7 gather_fusion.1
  306.2 3.2 %fusion.4 = f32[1,2048,256]{1,2,0:T(8,128)} fusion(f32[256,2048]{1,0:T(8,128)} %gather_fusion.1, f32[2048,256]{0,1:T(8,128)S(1)} %copy.17, pred[256]{0:T(512)(128)(4,1)S(1)} %compare_and_fusion), kind=kLoop, calls=%fused_computation.10 | loop fusion | flops 1048576 | bytes 6291712 | tf_op jit(solution)/shard_map/sub | solution.py:53
  309.4 2.9 copy.19
  312.3 0.0 copy-done.1
  (3 shorter events, 0.0 us)
Async XLA Ops:
  0.0 2.7 copy-start
  0.0 96.8 %copy-start.3 = (s32[1,16,20]{2,1,0:T(8,128)S(1)}, s32[1,16,20]{2,1,0:T(8,128)}, u32[]{:S(2)}) copy-start(s32[1,16,20]{2,1,0:T(8,128)} %param.9) | copy-start | bytes 3844
  4.4 13.4 %all-to-all-start = ((bf16[20,128,128]{2,1,0:T(8,128)(2,1)}), bf16[20,128,128]{2,1,0:T(8,128)(2,1)S(1)}, u32[]{:S(2)}, u32[]{:S(2)}) async-start(bf16[20,128,128]{2,1,0:T(8,128)(2,1)} %select_multiply_fusion), calls=%async_computation | async-start | bytes 1310720 | tf_op jit(solution)/shard_map/all_to_all | solution.py:26
  18.2 19.3 %collective-permute-start = (bf16[2560,128]{1,0:T(8,128)(2,1)S(1)}, bf16[2560,128]{1,0:T(8,128)(2,1)S(1)}, u32[]{:S(2)}, u32[]{:S(2)}) collective-permute-start(bf16[2560,128]{1,0:T(8,128)(2,1)S(1)} %fusion.5), channel_id=1, source_target_pairs={{0,1},{1,2},{2,3},{3,4},{4,5},{5,6},{6,7},{7,0},{8,9},{9,10},{10,1... | collective-permute-start | bytes 1966088 | tf_op jit(solution)/shard_map/ppermute | solution.py:12
  37.5 27.3 %collective-permute-start.1 = (bf16[2560,128]{1,0:T(8,128)(2,1)S(1)}, bf16[2560,128]{1,0:T(8,128)(2,1)S(1)}, u32[]{:S(2)}, u32[]{:S(2)}) collective-permute-start(bf16[2560,128]{1,0:T(8,128)(2,1)S(1)} %collective-permute-done), channel_id=1, source_target_pairs={{0,1},{1,2},{2,3},{3,4},{4,5},{5,6},{6,7},{7,0},{8,9},{9,10},{10,1... | collective-permute-start | bytes 1966088 | tf_op jit(solution)/shard_map/ppermute | solution.py:12
  37.5 29.5 %collective-permute-start.4 = (bf16[2560,128]{1,0:T(8,128)(2,1)S(1)}, bf16[2560,128]{1,0:T(8,128)(2,1)S(1)}, u32[]{:S(2)}, u32[]{:S(2)}) collective-permute-start(bf16[2560,128]{1,0:T(8,128)(2,1)S(1)} %fusion.5), channel_id=1, source_target_pairs={{0,7},{1,0},{2,1},{3,2},{4,3},{5,4},{6,5},{7,6},{8,15},{9,8},{10,9... | collective-permute-start | bytes 1966088 | tf_op jit(solution)/shard_map/ppermute | solution.py:12
  64.8 29.7 %collective-permute-start.2 = (bf16[2560,128]{1,0:T(8,128)(2,1)S(1)}, bf16[2560,128]{1,0:T(8,128)(2,1)}, u32[]{:S(2)}, u32[]{:S(2)}) collective-permute-start(bf16[2560,128]{1,0:T(8,128)(2,1)S(1)} %collective-permute-done.1), channel_id=1, source_target_pairs={{0,1},{1,2},{2,3},{3,4},{4,5},{5,6},{6,7},{7,0},{8,9},{9,10},{10,1... | collective-permute-start | bytes 1966088 | tf_op jit(solution)/shard_map/ppermute | solution.py:12
  67.0 44.5 %collective-permute-start.5 = (bf16[2560,128]{1,0:T(8,128)(2,1)S(1)}, bf16[2560,128]{1,0:T(8,128)(2,1)S(1)}, u32[]{:S(2)}, u32[]{:S(2)}) collective-permute-start(bf16[2560,128]{1,0:T(8,128)(2,1)S(1)} %collective-permute-done.4), channel_id=1, source_target_pairs={{0,7},{1,0},{2,1},{3,2},{4,3},{5,4},{6,5},{7,6},{8,15},{9,8},{10,9... | collective-permute-start | bytes 1966088 | tf_op jit(solution)/shard_map/ppermute | solution.py:12
  94.5 18.8 %collective-permute-start.3 = (bf16[2560,128]{1,0:T(8,128)(2,1)}, bf16[2560,128]{1,0:T(8,128)(2,1)}, u32[]{:S(2)}, u32[]{:S(2)}) collective-permute-start(bf16[2560,128]{1,0:T(8,128)(2,1)} %collective-permute-done.2), channel_id=1, source_target_pairs={{0,1},{1,2},{2,3},{3,4},{4,5},{5,6},{6,7},{7,0},{8,9},{9,10},{10,1... | collective-permute-start | bytes 1966088 | tf_op jit(solution)/shard_map/ppermute | solution.py:12
  111.5 14.6 %collective-permute-start.6 = (bf16[2560,128]{1,0:T(8,128)(2,1)S(1)}, bf16[2560,128]{1,0:T(8,128)(2,1)S(1)}, u32[]{:S(2)}, u32[]{:S(2)}) collective-permute-start(bf16[2560,128]{1,0:T(8,128)(2,1)S(1)} %collective-permute-done.5), channel_id=1, source_target_pairs={{0,7},{1,0},{2,1},{3,2},{4,3},{5,4},{6,5},{7,6},{8,15},{9,8},{10,9... | collective-permute-start | bytes 1966088 | tf_op jit(solution)/shard_map/ppermute | solution.py:12
  127.0 7.8 %copy-start.2 = (bf16[1,2048,2560]{1,2,0:T(8,128)(2,1)S(1)}, bf16[1,2048,2560]{1,2,0:T(8,128)(2,1)}, u32[]{:S(2)}) copy-start(bf16[1,2048,2560]{1,2,0:T(8,128)(2,1)} %copy.13) | copy-start | bytes 31457284
  205.8 8.3 %copy-start.4 = (s32[1,1,256]{2,1,0:T(1,128)S(1)}, s32[1,1,256]{2,1,0:T(1,128)}, u32[]{:S(2)}) copy-start(s32[1,1,256]{2,1,0:T(1,128)} %param.15) | copy-start | bytes 3076
  205.8 54.9 %all-to-all-start.1 = ((bf16[4,2,262144]{2,1,0:T(2,128)(2,1)}), bf16[4,2,262144]{2,1,0:T(2,128)(2,1)}, u32[]{:S(2)}, u32[]{:S(2)}) async-start(bf16[4,2,262144]{2,1,0:T(2,128)(2,1)} %reshape.163), calls=%async_computation.1 | async-start | bytes 8388608 | tf_op jit(solution)/shard_map/all_to_all | solution.py:47
  303.5 8.8 %copy-start.1 = (bf16[1,1,20,128,128]{4,3,2,1,0:T(8,128)(2,1)S(1)}, bf16[1,1,20,128,128]{4,3,2,1,0:T(8,128)(2,1)}, u32[]{:S(2)}) copy-start(bf16[1,1,20,128,128]{4,3,2,1,0:T(8,128)(2,1)} %param.10) | copy-start | bytes 1966084
where the time goes:
time: 315 us; the launch traced here: 312 us
  waiting for transfers between devices  110 us (35%)
  local copies, waits for them, and re-layouts  96.5 us (31%)
  other arithmetic  47.4 us (15%)
  starting transfers between devices  40.8 us (13%)
  matrix products  17 us (5%)
    ppermute x7, waiting for transfers between devices, passed_along(): return lax.ppermute(value, axis, pairs)  55.5 us
    all_to_all x1, waiting for transfers between devices, shards(): lax.all_to_all(product_block[None], 'grp', split_axis=2, concat_axis=0, t...  46.6 us
    unnamed x21, local copies, waits for them, and re-layouts  38.6 us
    ppermute x7, starting transfers between devices, passed_along(): return lax.ppermute(value, axis, pairs)  28.9 us
    unnamed x2, other arithmetic  27.4 us
    convert_element_type x1, local copies, waits for them, and re-layouts, shards(): returned.astype(jnp.float32)  21.4 us
    broadcast_in_dim x1, local copies, waits for them, and re-layouts, shards(): product_block[None]  20.6 us
    dot_general x1, matrix products, shards(): jnp.dot(masked, band_matrix, preferred_element_type=jnp.float32)  17 us
  transfers between devices with their start and end apart: 9, of which 6 were waited for; matrix products, arithmetic and copies ran while one was open for 8% of the time, Pallas kernels for 0%

commit v1 on v0

v1 whole, which is shorter than its diff:
```python
import functools

import jax
import jax.numpy as jnp
from jax import lax
from jax.experimental import pallas as pl
from jax.experimental.pallas import tpu as pltpu
from jax.sharding import PartitionSpec as P

BAND = 8
MESH = pl.DeviceIdType.MESH


def kernel(
    groups, blocks, gen_hbm, mask_ref, tiles_ref, order_ref, phase_ref, occ_ref, sign_ref, perm_ref,
    out_ref,
    eta, outgoing, arrived, band, prod, recv1, send2, recv2, total,
    gen_sem, ex_send, ex_recv, ring_send, ring_recv, p1_send, p1_recv, p2_send, p2_recv,
):
    tile = tiles_ref.shape[-1]
    tile_count = tiles_ref.shape[2]
    rows = eta.shape[0]
    chunk_tiles = tile_count // groups
    chunk = chunk_tiles * tile
    half = BAND // 2
    whole_ring = blocks == BAND
    g = lax.axis_index("grp")
    b = lax.axis_index("blk")
    y, k = g // 2, g % 2
    partner = y * 2 + 1 - k
    across = ((y + 1) % 2) * 2 + k

    if whole_ring:
        here = (b % 2) * (blocks - 1 - b // 2) + (1 - b % 2) * (b // 2)

        def at(pos):
            pos = (pos + 2 * blocks) % blocks
            far = pos // (blocks // 2)
            return far * (2 * (blocks - 1 - pos) + 1) + (1 - far) * 2 * pos
    else:
        here = b

        def at(pos):
            return (pos + 2 * blocks) % blocks

    def chunks_of(direction, step):
        if step < half:
            return range(groups)
        if whole_ring:
            return range(groups // 2) if direction == 0 else range(groups // 2, groups)
        return range(groups) if direction == 0 else range(0)

    neighbours = (at(here + 1), at(here - 1))

    def owner(j):
        return ((y + j // 2) % (groups // 2)) * 2 + (k + j) % 2

    row_blocks = rows // tile

    def load(i):
        r = pl.ds(i * tile, tile)
        return pltpu.make_async_copy(gen_hbm.at[0, r], eta.at[r], gen_sem.at[i])

    for i in range(row_blocks):
        load(i).start()

    barrier = pltpu.get_barrier_semaphore()
    for other in neighbours:
        pl.semaphore_signal(barrier, inc=1, device_id=(g, other), device_id_type=MESH)
    for j in range(1, groups):
        pl.semaphore_signal(barrier, inc=1, device_id=(owner(j), b), device_id_type=MESH)

    def fill(group, slot):
        for s in range(chunk_tiles):
            q = group * chunk_tiles + s
            phase = (1 - 2 * phase_ref[0, 0, q]).astype(jnp.float32)
            picked = tiles_ref[0, 0, order_ref[0, 0, q]].astype(jnp.float32) * phase
            outgoing[slot, pl.ds(s * tile, tile), :] = picked.astype(jnp.bfloat16)

    def exchange(j):
        return pltpu.make_async_remote_copy(
            outgoing.at[j], arrived.at[j], ex_send.at[j], ex_recv.at[j],
            device_id=(owner(j), b), device_id_type=MESH,
        )

    def scale(j, source):
        o = owner(j)
        for s in range(chunk_tiles):
            start = pl.multiple_of(o * chunk + s * tile, tile)
            occ = jnp.broadcast_to(occ_ref[0:1, pl.ds(start, tile)], (tile, tile)).T
            value = source[j, pl.ds(s * tile, tile), :].astype(jnp.float32)
            band[b % BAND, pl.ds(start, tile), :] = (occ * value).astype(jnp.bfloat16)

    def hop(direction, step, j):
        moved = step - 1 if direction == 0 else 1 - step
        block = at(here - moved)
        r = pl.ds(pl.multiple_of(owner(j) * chunk, tile), chunk)
        piece = band.at[block % BAND, r]
        return pltpu.make_async_remote_copy(
            piece, piece, ring_send.at[direction, step, j], ring_recv.at[direction, step, j],
            device_id=(g, neighbours[direction]), device_id_type=MESH,
        )

    def landed(direction, step, j):
        moved = step if direction == 0 else -step
        block = at(here - moved)
        r = pl.ds(pl.multiple_of(owner(j) * chunk, tile), chunk)
        piece = band.at[block % BAND, r]
        return pltpu.make_async_remote_copy(
            piece, piece, ring_send.at[direction, step, j], ring_recv.at[direction, step, j],
            device_id=(g, neighbours[direction]), device_id_type=MESH,
        )

    for j in range(groups):
        fill(owner(j), j)
    scale(0, outgoing)
    pl.semaphore_wait(barrier, groups + 1)
    for j in (2, 3, 1):
        exchange(j).start()
    for direction in range(2):
        hop(direction, 1, 0).start()
    for j in range(1, groups):
        exchange(j).wait_recv()
        scale(j, arrived)
        for direction in range(2):
            hop(direction, 1, j).start()

    for i in range(row_blocks):
        load(i).wait()

    @pl.loop(0, row_blocks)
    def _(i):
        r = pl.ds(pl.multiple_of(i * tile, tile), tile)
        for t in range(tile_count):
            c = pl.ds(t * tile, tile)
            keep = mask_ref[0, i, t].astype(jnp.float32).astype(jnp.bfloat16)
            eta[r, c] = eta[r, c] * keep

    def place(block):
        return (block - b + half + blocks) % blocks

    def to_partner(p):
        return pltpu.make_async_remote_copy(
            prod.at[p], recv1.at[p], p1_send.at[p], p1_recv.at[p],
            device_id=(partner, b), device_id_type=MESH,
        )

    def to_across(h):
        return pltpu.make_async_remote_copy(
            send2.at[h], recv2.at[h], p2_send.at[h], p2_recv.at[h],
            device_id=(across, b), device_id_type=MESH,
        )

    step_rows = 256

    def multiply(pair):
        places = [place(c) for c in pair]
        signs = [(1 - 2 * sign_ref[p // 2, g]).astype(jnp.float32) for p in places]

        @pl.loop(0, rows // step_rows)
        def _(m):
            r = pl.ds(pl.multiple_of(m * step_rows, step_rows), step_rows)
            right = jnp.concatenate([band[c % BAND] for c in pair], axis=1)
            value = jnp.dot(eta[r, :], right, preferred_element_type=jnp.float32)
            for n in range(2):
                part = value[:, n * tile:(n + 1) * tile] * signs[n]
                prod[places[n], r, :] = part.astype(jnp.bfloat16)

        for p in places:
            @pl.when((p // 2) % 2 != k)
            def _():
                to_partner(p).start()
        return places

    def combine(places):
        for p in places:
            h = p % 2

            @pl.when((p // 2) % 2 == k)
            def _():
                to_partner(p).wait_recv()

                @pl.when(p // 4 != y)
                def _():
                    @pl.loop(0, rows // step_rows)
                    def _(m):
                        r = pl.ds(pl.multiple_of(m * step_rows, step_rows), step_rows)
                        both = prod[p, r, :].astype(jnp.float32) + recv1[p, r, :].astype(jnp.float32)
                        send2[h, r, :] = both.astype(jnp.bfloat16)
                    to_across(h).start()

                @pl.when(p // 4 == y)
                def _():
                    @pl.loop(0, rows // step_rows)
                    def _(m):
                        r = pl.ds(pl.multiple_of(m * step_rows, step_rows), step_rows)
                        both = prod[p, r, :].astype(jnp.float32) + recv1[p, r, :].astype(jnp.float32)
                        total[h, r, :] = both

    waiting = []
    for step in range(1, half + 1):
        for j in range(groups):
            for direction in range(2):
                if j in chunks_of(direction, step):
                    landed(direction, step, j).wait_recv()
                    if step < half and j in chunks_of(direction, step + 1):
                        hop(direction, step + 1, j).start()
        if step < half:
            pair = (at(here - step), at(here + step))
        else:
            pair = (b, at(here - step))
        places = multiply(pair)
        for earlier in waiting:
            combine(earlier)
        waiting = [places]
    for earlier in waiting:
        combine(earlier)

    permutation = jnp.broadcast_to(perm_ref[0, 0:1, :], (2 * tile, 2 * tile))
    chosen = lax.broadcasted_iota(jnp.int32, (2 * tile, 2 * tile), 0) == permutation
    swap = jnp.where(chosen, 1.0, 0.0).astype(jnp.bfloat16)
    for h in range(2):
        to_across(h).wait_recv()

    @pl.loop(0, rows // step_rows)
    def _(m):
        r = pl.ds(pl.multiple_of(m * step_rows, step_rows), step_rows)
        summed = jnp.concatenate(
            [total[h, r, :] + recv2[h, r, :].astype(jnp.float32) for h in range(2)], axis=1
        )
        high = summed.astype(jnp.bfloat16)
        low = (summed - high.astype(jnp.float32)).astype(jnp.bfloat16)
        moved = jnp.dot(high, swap, preferred_element_type=jnp.float32) + jnp.dot(
            low, swap, preferred_element_type=jnp.float32
        )
        out_ref[0, r, :] = summed - moved

    for j in range(1, groups):
        exchange(j).wait_send()
    for step in range(1, half + 1):
        for direction in range(2):
            for j in chunks_of(direction, step):
                hop(direction, step, j).wait_send()
    for p in range(BAND):
        @pl.when((p // 2) % 2 != k)
        def _():
            to_partner(p).wait_send()
    for h in range(2):
        to_across(h).wait_send()


def solution(mesh):
    groups, blocks = mesh.shape["grp"], mesh.shape["blk"]

    def shards(
        generator, eta_mask, pair_tiles, tile_order, tile_phase, occupation, channel_sign, swap_perm
    ):
        tile = pair_tiles.shape[-1]
        rows, width = generator.shape[1:]
        columns = BAND * tile // groups
        bf16 = jnp.bfloat16
        vmem = pl.BlockSpec(memory_space=pltpu.VMEM)
        smem = pl.BlockSpec(memory_space=pltpu.SMEM)
        dma = pltpu.SemaphoreType.DMA
        chunk = width // groups
        ring = (2, BAND // 2 + 1, groups)
        return pl.pallas_call(
            functools.partial(kernel, groups, blocks),
            out_shape=jax.ShapeDtypeStruct((1, rows, columns), jnp.float32),
            in_specs=[pl.BlockSpec(memory_space=pl.ANY), smem, vmem, smem, smem, vmem, smem, vmem],
            out_specs=vmem,
            scratch_shapes=[
                pltpu.VMEM((rows, width), bf16),
                pltpu.VMEM((groups, chunk, tile), bf16),
                pltpu.VMEM((groups, chunk, tile), bf16),
                pltpu.VMEM((BAND, width, tile), bf16),
                pltpu.VMEM((BAND, rows, tile), bf16),
                pltpu.VMEM((BAND, rows, tile), bf16),
                pltpu.VMEM((2, rows, tile), bf16),
                pltpu.VMEM((2, rows, tile), bf16),
                pltpu.VMEM((2, rows, tile), jnp.float32),
                dma((rows // tile,)),
                dma((groups,)),
                dma((groups,)),
                dma(ring),
                dma(ring),
                dma((BAND,)),
                dma((BAND,)),
                dma((2,)),
                dma((2,)),
            ],
            compiler_params=pltpu.CompilerParams(
                collective_id=0, has_side_effects=True, vmem_limit_bytes=60 * 1024 * 1024
            ),
        )(generator, eta_mask, pair_tiles, tile_order, tile_phase, occupation, channel_sign, swap_perm)

    return jax.shard_map(
        shards,
        mesh=mesh,
        in_specs=(
            P("grp", "blk", None),
            P("grp", "blk", None),
            P("grp", "blk", None, None, None),
            P("grp", "blk", None),
            P("grp", "blk", None),
            P("grp", None),
            P(),
            P("grp", "blk", None),
        ),
        out_specs=P("grp", "blk", None),
        check_vma=False,
    )
```

time: 315 us -> 88.8 us (0.28)
  the two profiles are of different devices: /device:TPU:1 before, /device:TPU:30 now
where the time goes in v1:
time: 88.8 us; the launch traced here: 88.6 us
  Pallas kernels  85.6 us (96%)
  local copies, waits for them, and re-layouts  3.05 us (3%)
    pallas_call x1, Pallas kernels, shards(): pl.pallas_call(functools.partial(kernel, groups, blocks), out_shape=jax.S...  85.6 us
    unnamed x1, local copies, waits for them, and re-layouts  3.05 us

profile of v1, /device:TPU:30, one launch (start us, length us, event | category | flops | bytes accessed | tf_op | source)
XLA Modules:
  0.0 88.6 jit_solution(12769363814469321451)
XLA Ops:
  0.0 85.6 %shard_map.82 = f32[1,2048,256]{2,1,0:T(8,128)} custom-call(bf16[1,2048,2560]{2,1,0:T(8,128)(2,1)} %gen_hbm.1, s32[1,16,20]{2,1,0:T(8,128)} %mask_ref.1, bf16[1,1,20,128,128]{4,3,2,1,0:T(8,128)(2,1)} %tiles_ref.1, s32[1,1,20]{2,1,0:T(1,128)} %order_ref.1, s32[1,1,20]{2,1,0:T(1,128)} %phase_ref.1, f32[1,2560]{1,0:T(1,128)} %occ_ref.1, s32[4,4]{1,0:T(4,128)} %sign_ref.1, ...), custom_call_target="tpu_custom_call" | custom-call | tf_op jit(solution)/shard_map/pallas_call | solution.py:267
  85.6 3.0 %copy.10 = f32[1,2048,256]{2,1,0:T(8,128)} copy(f32[1,2048,256]{2,1,0:T(8,128)} %shard_map.82) | data formatting | bytes 4194304

commit v2 on v1

--- a/solution.py
+++ b/solution.py
@@ -14,7 +14,7 @@
 def kernel(
     groups, blocks, gen_hbm, mask_ref, tiles_ref, order_ref, phase_ref, occ_ref, sign_ref, perm_ref,
     out_ref,
-    eta, outgoing, arrived, band, prod, recv1, send2, recv2, total,
+    eta, outgoing, arrived, band, prod, recv1, send2, recv2, total, partial,
     gen_sem, ex_send, ex_recv, ring_send, ring_recv, p1_send, p1_recv, p2_send, p2_recv,
 ):
     tile = tiles_ref.shape[-1]
@@ -47,7 +47,7 @@
         if step < half:
             return range(groups)
         if whole_ring:
-            return range(groups // 2) if direction == 0 else range(groups // 2, groups)
+            return range(direction, groups, 2)
         return range(groups) if direction == 0 else range(0)
 
     neighbours = (at(here + 1), at(here - 1))
@@ -111,91 +111,128 @@
             device_id=(g, neighbours[direction]), device_id_type=MESH,
         )
 
-    for j in range(groups):
-        fill(owner(j), j)
+    fill(owner(0), 0)
     scale(0, outgoing)
     pl.semaphore_wait(barrier, groups + 1)
-    for j in (2, 3, 1):
-        exchange(j).start()
     for direction in range(2):
         hop(direction, 1, 0).start()
+    for j in (2, 3, 1):
+        fill(owner(j), j)
+        exchange(j).start()
+
+    def mask_rows(first, last):
+        for i in range(first, last):
+            load(i).wait()
+
+        @pl.loop(first, last)
+        def _(i):
+            r = pl.ds(pl.multiple_of(i * tile, tile), tile)
+            for t in range(tile_count):
+                c = pl.ds(t * tile, tile)
+                keep = mask_ref[0, i, t].astype(jnp.float32).astype(jnp.bfloat16)
+                eta[r, c] = eta[r, c] * keep
+
     for j in range(1, groups):
         exchange(j).wait_recv()
         scale(j, arrived)
         for direction in range(2):
             hop(direction, 1, j).start()
-
-    for i in range(row_blocks):
-        load(i).wait()
-
-    @pl.loop(0, row_blocks)
-    def _(i):
-        r = pl.ds(pl.multiple_of(i * tile, tile), tile)
-        for t in range(tile_count):
-            c = pl.ds(t * tile, tile)
-            keep = mask_ref[0, i, t].astype(jnp.float32).astype(jnp.bfloat16)
-            eta[r, c] = eta[r, c] * keep
+        if j < groups - 1:
+            mask_rows((j - 1) * row_blocks // (groups - 2), j * row_blocks // (groups - 2))
 
     def place(block):
         return (block - b + half + blocks) % blocks
 
-    def to_partner(p):
-        return pltpu.make_async_remote_copy(
-            prod.at[p], recv1.at[p], p1_send.at[p], p1_recv.at[p],
+    slices = row_blocks // 4
+    step_rows = rows // slices
+
+    def rows_of(m):
+        return pl.ds(pl.multiple_of(m * step_rows, step_rows), step_rows)
+
+    def to_partner(p, m):
+        r = rows_of(m)
+        return pltpu.make_async_remote_copy(
+            prod.at[p, r], recv1.at[p, r], p1_send.at[p, m], p1_recv.at[p, m],
             device_id=(partner, b), device_id_type=MESH,
         )
 
-    def to_across(h):
-        return pltpu.make_async_remote_copy(
-            send2.at[h], recv2.at[h], p2_send.at[h], p2_recv.at[h],
+    def to_across(h, m):
+        r = rows_of(m)
+        return pltpu.make_async_remote_copy(
+            send2.at[h, r], recv2.at[h, r], p2_send.at[h, m], p2_recv.at[h, m],
             device_id=(across, b), device_id_type=MESH,
         )
 
-    step_rows = 256
+    def sign(p):
+        return (1 - 2 * sign_ref[p // 2, g]).astype(jnp.float32)
+
+    def hand_over(p, m):
+        @pl.when((p // 2) % 2 != k)
+        def _():
+            to_partner(p, m).start()
 
     def multiply(pair):
         places = [place(c) for c in pair]
-        signs = [(1 - 2 * sign_ref[p // 2, g]).astype(jnp.float32) for p in places]
-
-        @pl.loop(0, rows // step_rows)
+        signs = [sign(p) for p in places]
+
+        @pl.loop(0, slices)
         def _(m):
-            r = pl.ds(pl.multiple_of(m * step_rows, step_rows), step_rows)
+            r = rows_of(m)
             right = jnp.concatenate([band[c % BAND] for c in pair], axis=1)
             value = jnp.dot(eta[r, :], right, preferred_element_type=jnp.float32)
-            for n in range(2):
+            for n, p in enumerate(places):
                 part = value[:, n * tile:(n + 1) * tile] * signs[n]
-                prod[places[n], r, :] = part.astype(jnp.bfloat16)
-
-        for p in places:
-            @pl.when((p // 2) % 2 != k)
+                prod[p, r, :] = part.astype(jnp.bfloat16)
+            for p in places:
+                hand_over(p, m)
+        return places
+
+    def half_columns(n):
+        span = groups // 2 * chunk
+        return pl.ds(pl.multiple_of(((y + n) % 2) * span, tile), span)
+
+    def multiply_first(c):
+        columns = half_columns(0)
+
+        @pl.loop(0, slices)
+        def _(m):
+            r = rows_of(m)
+            partial[r, :] = jnp.dot(
+                eta[r, columns], band[c % BAND, columns, :], preferred_element_type=jnp.float32
+            )
+
+    def multiply_rest(c, p, m):
+        columns = half_columns(1)
+        r = rows_of(m)
+        value = partial[r, :] + jnp.dot(
+            eta[r, columns], band[c % BAND, columns, :], preferred_element_type=jnp.float32
+        )
+        prod[p, r, :] = (value * sign(p)).astype(jnp.bfloat16)
+        hand_over(p, m)
+
+    def combine_slice(p, m):
+        h = p % 2
+
+        @pl.when((p // 2) % 2 == k)
+        def _():
+            r = rows_of(m)
+            to_partner(p, m).wait_recv()
+            both = prod[p, r, :].astype(jnp.float32) + recv1[p, r, :].astype(jnp.float32)
+
+            @pl.when(p // 4 != y)
             def _():
-                to_partner(p).start()
-        return places
+                send2[h, r, :] = both.astype(jnp.bfloat16)
+                to_across(h, m).start()
+
+            @pl.when(p // 4 == y)
+            def _():
+                total[h, r, :] = both
 
     def combine(places):
         for p in places:
-            h = p % 2
-
-            @pl.when((p // 2) % 2 == k)
-            def _():
-                to_partner(p).wait_recv()
-
-                @pl.when(p // 4 != y)
-                def _():
-                    @pl.loop(0, rows // step_rows)
-                    def _(m):
-                        r = pl.ds(pl.multiple_of(m * step_rows, step_rows), step_rows)
-                        both = prod[p, r, :].astype(jnp.float32) + recv1[p, r, :].astype(jnp.float32)
-                        send2[h, r, :] = both.astype(jnp.bfloat16)
-                    to_across(h).start()
-
-                @pl.when(p // 4 == y)
-                def _():
-                    @pl.loop(0, rows // step_rows)
-                    def _(m):
-                        r = pl.ds(pl.multiple_of(m * step_rows, step_rows), step_rows)
-                        both = prod[p, r, :].astype(jnp.float32) + recv1[p, r, :].astype(jnp.float32)
-                        total[h, r, :] = both
+            @pl.loop(0, slices)
+            def _(m):
+                combine_slice(p, m)
 
     waiting = []
     for step in range(1, half + 1):
@@ -205,26 +242,40 @@
                     landed(direction, step, j).wait_recv()
                     if step < half and j in chunks_of(direction, step + 1):
                         hop(direction, step + 1, j).start()
+            if j == groups // 2 - 1:
+                if step == 1:
+                    own = multiply((b,))
+                else:
+                    for places in waiting:
+                        combine(places)
+                    waiting = []
+                if step == half:
+                    multiply_first(at(here - step))
         if step < half:
             pair = (at(here - step), at(here + step))
-        else:
-            pair = (b, at(here - step))
-        places = multiply(pair)
-        for earlier in waiting:
-            combine(earlier)
-        waiting = [places]
-    for earlier in waiting:
-        combine(earlier)
+            waiting.append(multiply(pair))
+            if step == 1:
+                waiting.insert(0, own)
+
+    last = at(here - half)
+    last_place = place(last)
+    multiply_rest(last, last_place, 0)
+
+    @pl.loop(1, slices)
+    def _(m):
+        multiply_rest(last, last_place, m)
+        combine_slice(last_place, m - 1)
+    combine_slice(last_place, slices - 1)
 
     permutation = jnp.broadcast_to(perm_ref[0, 0:1, :], (2 * tile, 2 * tile))
     chosen = lax.broadcasted_iota(jnp.int32, (2 * tile, 2 * tile), 0) == permutation
     swap = jnp.where(chosen, 1.0, 0.0).astype(jnp.bfloat16)
-    for h in range(2):
-        to_across(h).wait_recv()
-
-    @pl.loop(0, rows // step_rows)
+
+    @pl.loop(0, slices)
     def _(m):
-        r = pl.ds(pl.multiple_of(m * step_rows, step_rows), step_rows)
+        r = rows_of(m)
+        for h in range(2):
+            to_across(h, m).wait_recv()
         summed = jnp.concatenate(
             [total[h, r, :] + recv2[h, r, :].astype(jnp.float32) for h in range(2)], axis=1
         )
@@ -244,9 +295,11 @@
     for p in range(BAND):
         @pl.when((p // 2) % 2 != k)
         def _():
-            to_partner(p).wait_send()
+            for m in range(slices):
+                to_partner(p, m).wait_send()
     for h in range(2):
-        to_across(h).wait_send()
+        for m in range(slices):
+            to_across(h, m).wait_send()
 
 
 def solution(mesh):
@@ -263,6 +316,7 @@
         smem = pl.BlockSpec(memory_space=pltpu.SMEM)
         dma = pltpu.SemaphoreType.DMA
         chunk = width // groups
+        slices = rows // tile // 4
         ring = (2, BAND // 2 + 1, groups)
         return pl.pallas_call(
             functools.partial(kernel, groups, blocks),
@@ -279,15 +333,16 @@
                 pltpu.VMEM((2, rows, tile), bf16),
                 pltpu.VMEM((2, rows, tile), bf16),
                 pltpu.VMEM((2, rows, tile), jnp.float32),
+                pltpu.VMEM((rows, tile), jnp.float32),
                 dma((rows // tile,)),
                 dma((groups,)),
                 dma((groups,)),
                 dma(ring),
                 dma(ring),
-                dma((BAND,)),
-                dma((BAND,)),
-                dma((2,)),
-                dma((2,)),
+                dma((BAND, slices)),
+                dma((BAND, slices)),
+                dma((2, slices)),
+                dma((2, slices)),
             ],
             compiler_params=pltpu.CompilerParams(
                 collective_id=0, has_side_effects=True, vmem_limit_bytes=60 * 1024 * 1024

time: 88.8 us -> 76.9 us (0.87)
  the two profiles are of different devices: /device:TPU:30 before, /device:TPU:1 now
where the time goes in v2:
time: 76.9 us; the launch traced here: 76.7 us
  Pallas kernels  73.7 us (96%)
  local copies, waits for them, and re-layouts  3.05 us (4%)
    pallas_call x1, Pallas kernels, shards(): pl.pallas_call(functools.partial(kernel, groups, blocks), out_shape=jax.S...  73.7 us
    unnamed x1, local copies, waits for them, and re-layouts  3.05 us

profile of v2, /device:TPU:1, one launch (start us, length us, event | category | flops | bytes accessed | tf_op | source)
XLA Modules:
  0.0 76.7 jit_solution(4630213652777431437)
XLA Ops:
  0.0 73.7 %shard_map.82 = f32[1,2048,256]{2,1,0:T(8,128)} custom-call(bf16[1,2048,2560]{2,1,0:T(8,128)(2,1)} %gen_hbm.1, s32[1,16,20]{2,1,0:T(8,128)} %mask_ref.1, bf16[1,1,20,128,128]{4,3,2,1,0:T(8,128)(2,1)} %tiles_ref.1, s32[1,1,20]{2,1,0:T(1,128)} %order_ref.1, s32[1,1,20]{2,1,0:T(1,128)} %phase_ref.1, f32[1,2560]{1,0:T(1,128)} %occ_ref.1, s32[4,4]{1,0:T(4,128)} %sign_ref.1, ...), custom_call_target="tpu_custom_call" | custom-call | tf_op jit(solution)/shard_map/pallas_call | solution.py:321
  73.7 3.0 %copy.10 = f32[1,2048,256]{2,1,0:T(8,128)} copy(f32[1,2048,256]{2,1,0:T(8,128)} %shard_map.82) | data formatting | bytes 4194304

commit v3 on v2

--- a/solution.py
+++ b/solution.py
@@ -12,10 +12,10 @@
 
 
 def kernel(
-    groups, blocks, gen_hbm, mask_ref, tiles_ref, order_ref, phase_ref, occ_ref, sign_ref, perm_ref,
-    out_ref,
-    eta, outgoing, arrived, band, prod, recv1, send2, recv2, total, partial,
-    gen_sem, ex_send, ex_recv, ring_send, ring_recv, p1_send, p1_recv, p2_send, p2_recv,
+    groups, blocks, gen_hbm, mask_ref, tiles_ref, order_ref, phase_ref, occ_ref, sign_ref,
+    total_out, recv2,
+    eta, outgoing, arrived, band, prod, recv1, send2, total, partial,
+    gen_sem, ex_send, ex_recv, ring_send, ring_recv, p1_send, p1_recv, p2_send, p2_recv, out_sem,
 ):
     tile = tiles_ref.shape[-1]
     tile_count = tiles_ref.shape[2]
@@ -163,6 +163,10 @@
             device_id=(across, b), device_id_type=MESH,
         )
 
+    def keep_total(h, m):
+        r = rows_of(m)
+        return pltpu.make_async_copy(total.at[h, r], total_out.at[h, r], out_sem.at[h, m])
+
     def sign(p):
         return (1 - 2 * sign_ref[p // 2, g]).astype(jnp.float32)
 
@@ -191,24 +195,43 @@
         span = groups // 2 * chunk
         return pl.ds(pl.multiple_of(((y + n) % 2) * span, tile), span)
 
-    def multiply_first(c):
+    def right_of(pair, columns):
+        pieces = [band[c % BAND, columns, :] for c in pair]
+        return pieces[0] if len(pieces) == 1 else jnp.concatenate(pieces, axis=1)
+
+    def multiply_first(pair):
         columns = half_columns(0)
 
         @pl.loop(0, slices)
         def _(m):
             r = rows_of(m)
-            partial[r, :] = jnp.dot(
-                eta[r, columns], band[c % BAND, columns, :], preferred_element_type=jnp.float32
+            partial[r, pl.ds(0, len(pair) * tile)] = jnp.dot(
+                eta[r, columns], right_of(pair, columns), preferred_element_type=jnp.float32
             )
 
-    def multiply_rest(c, p, m):
+    def multiply_rest(pair):
         columns = half_columns(1)
-        r = rows_of(m)
-        value = partial[r, :] + jnp.dot(
-            eta[r, columns], band[c % BAND, columns, :], preferred_element_type=jnp.float32
-        )
-        prod[p, r, :] = (value * sign(p)).astype(jnp.bfloat16)
-        hand_over(p, m)
+        places = [place(c) for c in pair]
+        lag = 2
+
+        @pl.loop(0, slices + lag)
+        def _(m):
+            @pl.when(m < slices)
+            def _():
+                r = rows_of(m)
+                value = partial[r, pl.ds(0, len(pair) * tile)] + jnp.dot(
+                    eta[r, columns], right_of(pair, columns), preferred_element_type=jnp.float32
+                )
+                for n, p in enumerate(places):
+                    part = value[:, n * tile:(n + 1) * tile] * sign(p)
+                    prod[p, r, :] = part.astype(jnp.bfloat16)
+                for p in places:
+                    hand_over(p, m)
+
+            @pl.when(m >= lag)
+            def _():
+                for p in places:
+                    combine_slice(p, m - lag)
 
     def combine_slice(p, m):
         h = p % 2
@@ -227,6 +250,7 @@
             @pl.when(p // 4 == y)
             def _():
                 total[h, r, :] = both
+                keep_total(h, m).start()
 
     def combine(places):
         for p in places:
@@ -249,42 +273,24 @@
                     for places in waiting:
                         combine(places)
                     waiting = []
+                if step == half - 1:
+                    multiply_first((at(here - step), at(here + step)))
                 if step == half:
-                    multiply_first(at(here - step))
-        if step < half:
+                    multiply_first((at(here - step),))
+        if step < half - 1:
             pair = (at(here - step), at(here + step))
             waiting.append(multiply(pair))
             if step == 1:
                 waiting.insert(0, own)
-
-    last = at(here - half)
-    last_place = place(last)
-    multiply_rest(last, last_place, 0)
-
-    @pl.loop(1, slices)
-    def _(m):
-        multiply_rest(last, last_place, m)
-        combine_slice(last_place, m - 1)
-    combine_slice(last_place, slices - 1)
-
-    permutation = jnp.broadcast_to(perm_ref[0, 0:1, :], (2 * tile, 2 * tile))
-    chosen = lax.broadcasted_iota(jnp.int32, (2 * tile, 2 * tile), 0) == permutation
-    swap = jnp.where(chosen, 1.0, 0.0).astype(jnp.bfloat16)
-
-    @pl.loop(0, slices)
-    def _(m):
-        r = rows_of(m)
-        for h in range(2):
+        elif step == half - 1:
+            multiply_rest((at(here - step), at(here + step)))
+        else:
+            multiply_rest((at(here - step),))
+
+    for h in range(2):
+        for m in range(slices):
+            keep_total(h, m).wait()
             to_across(h, m).wait_recv()
-        summed = jnp.concatenate(
-            [total[h, r, :] + recv2[h, r, :].astype(jnp.float32) for h in range(2)], axis=1
-        )
-        high = summed.astype(jnp.bfloat16)
-        low = (summed - high.astype(jnp.float32)).astype(jnp.bfloat16)
-        moved = jnp.dot(high, swap, preferred_element_type=jnp.float32) + jnp.dot(
-            low, swap, preferred_element_type=jnp.float32
-        )
-        out_ref[0, r, :] = summed - moved
 
     for j in range(1, groups):
         exchange(j).wait_send()
@@ -302,6 +308,22 @@
             to_across(h, m).wait_send()
 
 
+def exchange_kernel(total_ref, other_ref, perm_ref, out_ref):
+    tile = total_ref.shape[2]
+    permutation = jnp.broadcast_to(perm_ref[0, 0:1, :], (2 * tile, 2 * tile))
+    chosen = lax.broadcasted_iota(jnp.int32, (2 * tile, 2 * tile), 0) == permutation
+    swap = jnp.where(chosen, 1.0, 0.0).astype(jnp.bfloat16)
+    summed = jnp.concatenate(
+        [total_ref[h] + other_ref[h].astype(jnp.float32) for h in range(2)], axis=1
+    )
+    high = summed.astype(jnp.bfloat16)
+    low = (summed - high.astype(jnp.float32)).astype(jnp.bfloat16)
+    moved = jnp.dot(high, swap, preferred_element_type=jnp.float32) + jnp.dot(
+        low, swap, preferred_element_type=jnp.float32
+    )
+    out_ref[0] = summed - moved
+
+
 def solution(mesh):
     groups, blocks = mesh.shape["grp"], mesh.shape["blk"]
 
@@ -318,11 +340,14 @@
         chunk = width // groups
         slices = rows // tile // 4
         ring = (2, BAND // 2 + 1, groups)
-        return pl.pallas_call(
+        total, other = pl.pallas_call(
             functools.partial(kernel, groups, blocks),
-            out_shape=jax.ShapeDtypeStruct((1, rows, columns), jnp.float32),
-            in_specs=[pl.BlockSpec(memory_space=pl.ANY), smem, vmem, smem, smem, vmem, smem, vmem],
-            out_specs=vmem,
+            out_shape=(
+                jax.ShapeDtypeStruct((2, rows, tile), jnp.float32),
+                jax.ShapeDtypeStruct((2, rows, tile), bf16),
+            ),
+            in_specs=[pl.BlockSpec(memory_space=pl.ANY), smem, vmem, smem, smem, vmem, smem],
+            out_specs=(pl.BlockSpec(memory_space=pl.ANY), pl.BlockSpec(memory_space=pl.ANY)),
             scratch_shapes=[
                 pltpu.VMEM((rows, width), bf16),
                 pltpu.VMEM((groups, chunk, tile), bf16),
@@ -331,9 +356,8 @@
                 pltpu.VMEM((BAND, rows, tile), bf16),
                 pltpu.VMEM((BAND, rows, tile), bf16),
                 pltpu.VMEM((2, rows, tile), bf16),
-                pltpu.VMEM((2, rows, tile), bf16),
                 pltpu.VMEM((2, rows, tile), jnp.float32),
-                pltpu.VMEM((rows, tile), jnp.float32),
+                pltpu.VMEM((rows, 2 * tile), jnp.float32),
                 dma((rows // tile,)),
                 dma((groups,)),
                 dma((groups,)),
@@ -343,11 +367,21 @@
                 dma((BAND, slices)),
                 dma((2, slices)),
                 dma((2, slices)),
+                dma((2, slices)),
             ],
             compiler_params=pltpu.CompilerParams(
                 collective_id=0, has_side_effects=True, vmem_limit_bytes=60 * 1024 * 1024
             ),
-        )(generator, eta_mask, pair_tiles, tile_order, tile_phase, occupation, channel_sign, swap_perm)
+        )(generator, eta_mask, pair_tiles, tile_order, tile_phase, occupation, channel_sign)
+        step = rows // slices
+        part = pl.BlockSpec((2, step, tile), lambda m: (0, m, 0))
+        return pl.pallas_call(
+            exchange_kernel,
+            grid=(slices,),
+            out_shape=jax.ShapeDtypeStruct((1, rows, columns), jnp.float32),
+            in_specs=[part, part, pl.BlockSpec((1, 1, columns), lambda m: (0, 0, 0))],
+            out_specs=pl.BlockSpec((1, step, columns), lambda m: (0, m, 0)),
+        )(total, other, swap_perm)
 
     return jax.shard_map(
         shards,

time: 76.9 us -> 76.6 us (level)
  local copies, waits for them, and re-layouts: 3.05 us -> 0 us
  Pallas kernels: 73.7 us -> 76.4 us
    unnamed x1 -> x0, local copies, waits for them, and re-layouts: 3.05 us -> none
    pallas_call x1 -> x2, Pallas kernels: 73.7 us -> 76.4 us  [the longest x1 71.8 us: shards(): pl.pallas_call(functools.partial(kernel, groups, blocks), out_shape=(jax....]
where the time goes in v3:
time: 76.6 us; the launch traced here: 76.4 us
  Pallas kernels  76.4 us (100%)
    pallas_call x1, Pallas kernels, shards(): pl.pallas_call(functools.partial(kernel, groups, blocks), out_shape=(jax....  71.8 us
    pallas_call x1, Pallas kernels, shards(): pl.pallas_call(exchange_kernel, grid=(slices,), out_shape=jax.ShapeDtypeS...  4.52 us

profile of v3, /device:TPU:1, one launch (start us, length us, event | category | flops | bytes accessed | tf_op | source)
XLA Modules:
  0.0 76.4 jit_solution(3789334977608183680)
XLA Ops:
  0.0 71.8 %shard_map.82 = (f32[2,2048,128]{2,1,0:T(8,128)}, bf16[2,2048,128]{2,1,0:T(8,128)(2,1)}) custom-call(bf16[1,2048,2560]{2,1,0:T(8,128)(2,1)} %gen_hbm.1, s32[1,16,20]{2,1,0:T(8,128)} %mask_ref.1, bf16[1,1,20,128,128]{4,3,2,1,0:T(8,128)(2,1)} %tiles_ref.1, s32[1,1,20]{2,1,0:T(1,128)} %order_ref.1, s32[1,1,20]{2,1,0:T(1,128)} %phase_ref.1, f32[1,2560]{1,0:T(1,128)} %occ_ref.1, ...), custom_call_target="tpu_custom_call" | custom-call | tf_op jit(solution)/shard_map/pallas_call | solution.py:343
  71.9 4.5 %shard_map.83 = f32[1,2048,256]{2,1,0:T(8,128)} custom-call(f32[2,2048,128]{2,1,0:T(8,128)} %get-tuple-element.7.total_ref, bf16[2,2048,128]{2,1,0:T(8,128)(2,1)} %get-tuple-element.8.other_ref, s32[1,1,256]{2,1,0:T(1,128)} %perm_ref.1), custom_call_target="tpu_custom_call" | custom-call | tf_op jit(solution)/shard_map/pallas_call | solution.py:378

commit v4 on v3

--- a/solution.py
+++ b/solution.py
@@ -310,11 +310,13 @@
 
 def exchange_kernel(total_ref, other_ref, perm_ref, out_ref):
     tile = total_ref.shape[2]
+    step = out_ref.shape[1]
+    r = pl.ds(pl.multiple_of(pl.program_id(0) * step, step), step)
     permutation = jnp.broadcast_to(perm_ref[0, 0:1, :], (2 * tile, 2 * tile))
     chosen = lax.broadcasted_iota(jnp.int32, (2 * tile, 2 * tile), 0) == permutation
     swap = jnp.where(chosen, 1.0, 0.0).astype(jnp.bfloat16)
     summed = jnp.concatenate(
-        [total_ref[h] + other_ref[h].astype(jnp.float32) for h in range(2)], axis=1
+        [total_ref[h, r, :] + other_ref[h, r, :].astype(jnp.float32) for h in range(2)], axis=1
     )
     high = summed.astype(jnp.bfloat16)
     low = (summed - high.astype(jnp.float32)).astype(jnp.bfloat16)
@@ -370,17 +372,17 @@
                 dma((2, slices)),
             ],
             compiler_params=pltpu.CompilerParams(
-                collective_id=0, has_side_effects=True, vmem_limit_bytes=60 * 1024 * 1024
+                collective_id=0, has_side_effects=True, vmem_limit_bytes=50 * 1024 * 1024
             ),
         )(generator, eta_mask, pair_tiles, tile_order, tile_phase, occupation, channel_sign)
         step = rows // slices
-        part = pl.BlockSpec((2, step, tile), lambda m: (0, m, 0))
         return pl.pallas_call(
             exchange_kernel,
             grid=(slices,),
             out_shape=jax.ShapeDtypeStruct((1, rows, columns), jnp.float32),
-            in_specs=[part, part, pl.BlockSpec((1, 1, columns), lambda m: (0, 0, 0))],
+            in_specs=[vmem, vmem, pl.BlockSpec((1, 1, columns), lambda m: (0, 0, 0))],
             out_specs=pl.BlockSpec((1, step, columns), lambda m: (0, m, 0)),
+            compiler_params=pltpu.CompilerParams(vmem_limit_bytes=24 * 1024 * 1024),
         )(total, other, swap_perm)
 
     return jax.shard_map(

time: 76.6 us -> 78.7 us (1.027)
  local copies, waits for them, and re-layouts: 0 us -> 4.48 us
  Pallas kernels: 76.4 us -> 73.9 us
    unnamed x0 -> x14, local copies, waits for them, and re-layouts: none -> 4.48 us
    pallas_call x1, Pallas kernels: 4.52 us -> 2.59 us  [shards(): pl.pallas_call(exchange_kernel, grid=(slices,), out_shape=jax.ShapeDtypeS...]
where the time goes in v4:
time: 78.7 us; the launch traced here: 78.4 us
  Pallas kernels  73.9 us (94%)
  local copies, waits for them, and re-layouts  4.48 us (6%)
    pallas_call x1, Pallas kernels, shards(): pl.pallas_call(functools.partial(kernel, groups, blocks), out_shape=(jax....  71.3 us
    unnamed x14, local copies, waits for them, and re-layouts  4.48 us
    pallas_call x1, Pallas kernels, shards(): pl.pallas_call(exchange_kernel, grid=(slices,), out_shape=jax.ShapeDtypeS...  2.59 us

profile of v4, /device:TPU:1, one launch (start us, length us, event | category | flops | bytes accessed | tf_op | source)
XLA Modules:
  0.0 78.4 jit_solution(16990299058698371297)
XLA Ops:
  0.0 0.0 copy-start
  0.0 1.1 %copy-done = bf16[1,1,20,128,128]{4,3,2,1,0:T(8,128)(2,1)S(1)} copy-done((bf16[1,1,20,128,128]{4,3,2,1,0:T(8,128)(2,1)S(1)}, bf16[1,1,20,128,128]{4,3,2,1,0:T(8,128)(2,1)}, u32[]{:S(2)}) %copy-start) | copy-done | bytes 655384
  1.1 0.0 copy-start.1
  1.1 0.7 copy-done.1
  1.8 0.0 copy-start.2
  1.8 0.7 copy-done.2
  2.5 0.0 copy-start.3
  2.5 0.7 copy-done.3
  3.2 0.0 copy-start.5
  3.2 0.7 copy-done.5
  3.8 0.0 copy-start.6
  3.8 0.7 copy-done.6
  4.5 0.0 copy-start.4
  4.5 71.3 %shard_map.82 = (f32[2,2048,128]{2,1,0:T(8,128)S(1)}, bf16[2,2048,128]{2,1,0:T(8,128)(2,1)S(1)}) custom-call(bf16[1,2048,2560]{2,1,0:T(8,128)(2,1)} %gen_hbm.1, s32[1,16,20]{2,1,0:T(8,128)S(1)} %copy-done.2, bf16[1,1,20,128,128]{4,3,2,1,0:T(8,128)(2,1)S(1)} %copy-done, s32[1,1,20]{2,1,0:T(1,128)S(1)} %copy-done.5, s32[1,1,20]{2,1,0:T(1,128)S(1)} %copy-done.6, ...), custom_call_target="tpu_custom_call" | custom-call | tf_op jit(solution)/shard_map/pallas_call | solution.py:345
  75.8 0.0 copy-done.4
  75.9 2.6 %shard_map.83 = f32[1,2048,256]{2,1,0:T(8,128)} custom-call(f32[2,2048,128]{2,1,0:T(8,128)S(1)} %get-tuple-element.7.total_ref, bf16[2,2048,128]{2,1,0:T(8,128)(2,1)S(1)} %get-tuple-element.8.other_ref, s32[1,1,256]{2,1,0:T(1,128)S(1)} %copy-done.4), custom_call_target="tpu_custom_call" | custom-call | tf_op jit(solution)/shard_map/pallas_call | solution.py:379
Async XLA Ops:
  0.0 1.1 %copy-start = (bf16[1,1,20,128,128]{4,3,2,1,0:T(8,128)(2,1)S(1)}, bf16[1,1,20,128,128]{4,3,2,1,0:T(8,128)(2,1)}, u32[]{:S(2)}) copy-start(bf16[1,1,20,128,128]{4,3,2,1,0:T(8,128)(2,1)} %tiles_ref.1) | copy-start | bytes 1966084
  1.1 0.7 copy-start.1
  1.8 0.7 copy-start.2
  2.5 0.7 copy-start.3
  3.2 0.7 copy-start.5
  3.8 0.7 copy-start.6
  4.5 71.4 %copy-start.4 = (s32[1,1,256]{2,1,0:T(1,128)S(1)}, s32[1,1,256]{2,1,0:T(1,128)}, u32[]{:S(2)}) copy-start(s32[1,1,256]{2,1,0:T(1,128)} %perm_ref.1) | copy-start | bytes 3076
